TPU v7x, 32 devices: a whole 2x2x4 slice. The times are simulated.
32 devices in a mesh: tp: 4 (over y, core), fsdp: 8 (over z, x).
Axes of the slice: x: 2, y: 2, z: 4, core: 2. Of those that a mesh axis runs over, the one named last changes fastest.
Arguments:
- momentum: float32 [8192, 28672], P('tp', 'fsdp'), may hold values from -6 to 6
- gradient: bfloat16 [8192, 28672], P('tp', 'fsdp'), may hold values from -6 to 6
- basis: float32 [28672, 512], P('fsdp', 'tp'), may hold values from -1 to 1
Outputs:
- new_momentum: float32 [8192, 28672], P('tp', 'fsdp')
- new_basis: float32 [28672, 512], P('fsdp', 'tp')
- left_factor: float32 [8192, 512], P(('tp', 'fsdp'))
All inputs are finite; a program needn't handle non-finite values.
Results may differ from a plain program's by a relative error of at most 0.0003.
Values sent between devices are 32-bit elements; how exact they have to be, the bound alone decides.
A program may use at most 192 MiB of HBM per device.

v0:
```python
import jax
import jax.numpy as jnp
from jax import lax
from jax.sharding import PartitionSpec as P

keep_rate = 0.95
tiny = 1e-06
high = lax.Precision.HIGHEST


def solve_right(left, gram):
    lower = jnp.linalg.cholesky(gram)
    return jax.scipy.linalg.solve_triangular(lower, left.T, lower=True).T


def local_gram(left):
    return jnp.dot(left.T, left, precision=high, preferred_element_type=jnp.float32)


def gram_over_rows(left):
    return lax.psum(local_gram(left), "tp")


def on_device(momentum, gradient, basis):
    tile = momentum + gradient.astype(jnp.float32)
    partial_value = jnp.dot(
        tile,
        lax.all_gather(basis, "tp", axis=1, tiled=True),
        precision=high,
        preferred_element_type=jnp.float32,
    )
    share_rows = tile.shape[0] // lax.axis_size("fsdp")
    whole = lax.psum(partial_value, "fsdp")
    for turn in range(2):
        whole = solve_right(whole, gram_over_rows(whole))
    own_left = lax.dynamic_slice_in_dim(whole, lax.axis_index("fsdp") * share_rows, share_rows, 0)
    partial_right = jnp.dot(tile.T, whole, precision=high, preferred_element_type=jnp.float32)
    mine = lax.psum_scatter(partial_right, "tp", scatter_dimension=1, tiled=True)
    squares = lax.psum(jnp.sum(mine * mine, axis=0), "fsdp")
    new_basis = mine / jnp.sqrt(squares + tiny)[None, :]
    full_right = lax.all_gather(mine, "tp", axis=1, tiled=True)
    new_momentum = tile - (1.0 - keep_rate) * jnp.dot(
        whole, full_right.T, precision=high, preferred_element_type=jnp.float32
    )
    return (new_momentum, new_basis, own_left)


def solution(mesh):
    placed = (P("tp", "fsdp"), P("tp", "fsdp"), P("fsdp", "tp"))
    return jax.shard_map(
        on_device,
        mesh=mesh,
        in_specs=placed,
        out_specs=(P("tp", "fsdp"), P("fsdp", "tp"), P(("tp", "fsdp"), None)),
        check_vma=False,
    )
```

profile of v0, /device:TPU:0, one launch (start us, length us, event | category | flops | bytes accessed | tf_op | source)
XLA Modules:
  0.0 1009.8 jit_solution(1744838277263823175)
XLA Ops:
  7.9 57.6 %all-gather.3.cloned.1.call-done = f32[3584,512]{1,0:T(8,128)} async-done(((f32[3584,128]{1,0:T(8,128)}), f32[3584,512]{1,0:T(8,128)}) %all-gather.3.cloned.1.call-update) | async-done | bytes 7340048 | tf_op jit(solution)/shard_map/all_gather | solution.py:28
  65.6 53.8 %fusion.1 = f32[2048,512]{1,0:T(8,128)} fusion(f32[3584,512]{1,0:T(8,128)} %all-gather.3.cloned.1.call-done, f32[2048,3584]{1,0:T(8,128)} %param.6, bf16[2048,3584]{1,0:T(8,128)(2,1)} %param.7), kind=kOutput, calls=%fused_computation.7 | convolution fusion | flops 45111836672 | bytes 55574528 | tf_op jit(solution)/shard_map/dot_general | solution.py:26
  119.4 156.5 %all-reduce.5.cloned.1.call-done = f32[2048,512]{1,0:T(8,128)} async-done(((f32[2048,512]{1,0:T(8,128)}), f32[2048,512]{1,0:T(8,128)}) %all-reduce.5.cloned.1.call-update) | async-done | bytes 4194320 | tf_op jit(solution)/shard_map/psum | solution.py:33
  275.9 11.4 %fusion.88 = f32[512,512]{0,1:T(8,128)} fusion(f32[2048,512]{1,0:T(8,128)} %all-reduce.5.cloned.1.call-done), kind=kOutput, calls=%fused_computation.151 | convolution fusion | flops 6442450944 | bytes 5242880 | tf_op jit(solution)/shard_map/dot_general | solution.py:17
  287.8 34.9 %all-reduce.7.cloned.1.call-done = f32[512,512]{0,1:T(8,128)} async-done(((f32[512,512]{0,1:T(8,128)}), f32[512,512]{0,1:T(8,128)}) %all-reduce.7.cloned.1.call-update) | async-done | bytes 1048592 | tf_op jit(solution)/shard_map/psum | solution.py:21
  325.8 11.7 %cholesky.286 = f32[128,128]{1,0:T(8,128)S(1)} custom-call(f32[128,128]{1,0:T(8,128)S(1)} %cholesky.426), custom_call_target="Cholesky" | custom-call | tf_op jit(solution)/shard_map/jit(cholesky)/cholesky | solution.py:12
  337.7 9.8 custom-call.27
  348.2 11.7 %cholesky.305 = f32[128,128]{1,0:T(8,128)S(1)} custom-call(f32[128,128]{1,0:T(8,128)S(1)} %cholesky.430), custom_call_target="Cholesky" | custom-call | tf_op jit(solution)/shard_map/jit(cholesky)/cholesky | solution.py:12
  359.9 10.0 custom-call.28
  370.5 11.7 %cholesky.326 = f32[128,128]{1,0:T(8,128)S(1)} custom-call(f32[128,128]{1,0:T(8,128)S(1)} %cholesky.435), custom_call_target="Cholesky" | custom-call | tf_op jit(solution)/shard_map/jit(cholesky)/cholesky | solution.py:12
  382.3 9.8 custom-call.29
  392.7 11.7 %cholesky.343 = f32[128,128]{1,0:T(8,128)S(1)} custom-call(f32[128,128]{1,0:T(8,128)S(1)} %convolution_subtract_fusion.9), custom_call_target="Cholesky" | custom-call | tf_op jit(solution)/shard_map/jit(cholesky)/cholesky | solution.py:12
  409.3 8.0 while.4
  417.3 39.3 %custom-call.30 = f32[4,128,128]{1,2,0:T(8,128)S(1)} custom-call(f32[4,128,128]{2,1,0:T(8,128)S(1)} %get-tuple-element.19), custom_call_target="InvertDiagBlocksLowerTriangular" | custom-call | tf_op jit(solution)/shard_map/jit(_solve_triangular)/triangular_solve | solution.py:13
  463.2 3.5 convolution_subtract_fusion.1
  467.9 5.7 fusion.25
  475.7 7.8 fusion.2
  483.7 36.7 %all-reduce.9.cloned.1.call-done = f32[512,512]{0,1:T(8,128)} async-done(((f32[512,512]{0,1:T(8,128)}), f32[512,512]{0,1:T(8,128)}) %all-reduce.9.cloned.1.call-update) | async-done | bytes 1048592 | tf_op jit(solution)/shard_map/psum | solution.py:21
  524.4 11.7 %cholesky.358 = f32[128,128]{1,0:T(8,128)S(1)} custom-call(f32[128,128]{1,0:T(8,128)S(1)} %cholesky.439), custom_call_target="Cholesky" | custom-call | tf_op jit(solution)/shard_map/jit(cholesky)/cholesky | solution.py:12
  536.3 9.8 custom-call.31
  548.6 11.7 %cholesky.377 = f32[128,128]{1,0:T(8,128)S(1)} custom-call(f32[128,128]{1,0:T(8,128)S(1)} %cholesky.443), custom_call_target="Cholesky" | custom-call | tf_op jit(solution)/shard_map/jit(cholesky)/cholesky | solution.py:12
  560.4 10.0 custom-call.32
  572.0 11.7 %cholesky.398 = f32[128,128]{1,0:T(8,128)S(1)} custom-call(f32[128,128]{1,0:T(8,128)S(1)} %cholesky.448), custom_call_target="Cholesky" | custom-call | tf_op jit(solution)/shard_map/jit(cholesky)/cholesky | solution.py:12
  583.7 9.8 custom-call.33
  595.0 11.7 %cholesky.415 = f32[128,128]{1,0:T(8,128)S(1)} custom-call(f32[128,128]{1,0:T(8,128)S(1)} %convolution_subtract_fusion.8), custom_call_target="Cholesky" | custom-call | tf_op jit(solution)/shard_map/jit(cholesky)/cholesky | solution.py:12
  613.5 11.7 %while.5 = (s32[]{:T(128)}, f32[512,512]{1,0:T(8,128)}, s32[4,2]{0,1:T(2,128)S(1)}, f32[4,128,128]{2,1,0:T(8,128)S(1)}, s32[]{:T(128)}) while((s32[]{:T(128)}, f32[512,512]{1,0:T(8,128)}, s32[4,2]{0,1:T(2,128)S(1)}, f32[4,128,128]{2,1,0:T(8,128)S(1)}, s32[]{:T(128)}) %tuple.74), condition=%wide.while_cond.clone, body=%wide.while_body.clone.sunk | while | flops 2 | bytes 131189 | solution.py:13
  625.2 39.3 %custom-call.34 = f32[4,128,128]{1,2,0:T(8,128)S(1)} custom-call(f32[4,128,128]{2,1,0:T(8,128)S(1)} %get-tuple-element.20), custom_call_target="InvertDiagBlocksLowerTriangular" | custom-call | tf_op jit(solution)/shard_map/jit(_solve_triangular)/triangular_solve | solution.py:13
  677.2 107.3 %fusion = f32[3584,512]{1,0:T(8,128)} fusion(f32[2048,3584]{1,0:T(8,128)} %param.6, bf16[2048,3584]{1,0:T(8,128)(2,1)} %param.7, f32[128,2048]{1,0:T(8,128)S(1)} %fusion.54, f32[128,2048]{1,0:T(8,128)S(1)} %fusion.55, f32[128,2048]{1,0:T(8,128)S(1)} %fusion.57, f32[128,2048]{1,0:T(8,128)S(1)} %fusion.58), kind=kOutput, calls=%fused_computation.6 | convolution fusion | flops 45114982400 | bytes 55574528 | tf_op jit(solution)/shard_map/dot_general | solution.py:37
  784.6 65.2 %reduce-scatter.2.cloned.1.call-done = f32[3584,128]{1,0:T(8,128)} async-done(((f32[3584,512]{1,0:T(8,128)}), f32[3584,128]{1,0:T(8,128)}) %reduce-scatter.2.cloned.1.call-update) | async-done | bytes 1835024 | tf_op jit(solution)/shard_map/reduce_scatter | solution.py:38
  856.2 21.4 %psum.31 = f32[128]{0:T(128)S(1)} all-reduce(f32[128]{0:T(128)S(1)} %multiply_reduce_fusion), channel_id=1, replica_groups=mesh['tp'=4,'fsdp'=8] {'fsdp'}, use_global_device_ids=true, to_apply=%region_13.16 | all-reduce | flops 128 | bytes 1024 | tf_op jit(solution)/shard_map/psum | solution.py:39
  880.4 24.1 %all-gather.5.cloned.1.call-done = f32[3584,512]{1,0:T(8,128)} async-done(((f32[3584,128]{1,0:T(8,128)}), f32[3584,512]{1,0:T(8,128)}) %all-gather.5.cloned.1.call-update) | async-done | bytes 7340048 | tf_op jit(solution)/shard_map/all_gather | solution.py:41
  904.5 98.3 %multiply_subtract_fusion = f32[2048,3584]{1,0:T(8,128)} fusion(f32[3584,512]{1,0:T(8,128)} %all-gather.5.cloned.1.call-done, f32[2048,3584]{1,0:T(8,128)} %param.6, bf16[2048,3584]{1,0:T(8,128)(2,1)} %param.7, f32[128,2048]{1,0:T(8,128)} %copy-done.2, f32[128,2048]{1,0:T(8,128)S(1)} %fusion.55, f32[128,2048]{1,0:T(8,128)S(1)} %fusion.57, ...), kind=kOutput, calls=%fused_computation.4 | convolution fusion | flops 45129662464 | bytes 84934656 | tf_op jit(solution)/shard_map/dot_general | solution.py:42
  (111 shorter events, 73.9 us)
Async XLA Ops:
  7.2 58.4 %all-gather.3.cloned.1.call-start = ((), (), s32[]{:S(2)}) async-start(), calls=%async_computation.1 | async-start | bytes 9175040 | tf_op jit(solution)/shard_map/all_gather | solution.py:28
  7.9 268.0 %all-reduce.5.cloned.1.call-start = ((), (), s32[]{:S(2)}) async-start(), calls=%async_computation.2 | async-start | bytes 8388608 | tf_op jit(solution)/shard_map/psum | solution.py:33
  119.4 203.4 %all-reduce.7.cloned.1.call-start = ((), (), s32[]{:S(2)}) async-start(), calls=%async_computation.3 | async-start | bytes 2097152 | tf_op jit(solution)/shard_map/psum | solution.py:21
  287.3 233.1 %all-reduce.9.cloned.1.call-start = ((), (), s32[]{:S(2)}) async-start(), calls=%async_computation.4 | async-start | bytes 2097152 | tf_op jit(solution)/shard_map/psum | solution.py:21
  456.7 6.6 copy-start
  467.9 6.9 copy-start.1
  474.7 1.0 copy-start.3
  483.5 366.2 %reduce-scatter.2.cloned.1.call-start = ((), (), s32[]{:S(2)}) async-start(), calls=%async_computation.5 | async-start | bytes 9175040 | tf_op jit(solution)/shard_map/reduce_scatter | solution.py:38
  523.4 1.0 copy-start.5
  667.5 4.7 copy-start.4
  676.2 1.0 copy-start.2
  784.5 119.9 %all-gather.5.cloned.1.call-start = ((), (), s32[]{:S(2)}) async-start(), calls=%async_computation.6 | async-start | bytes 9175040 | tf_op jit(solution)/shard_map/all_gather | solution.py:41
Sparse Core Ops, SparseCore 0:
  9.5 56.0 all-gather.2
  119.5 156.3 all-reduce.4
  287.4 35.2 all-reduce.6
  483.6 36.7 all-reduce.8
  784.6 65.0 reduce-scatter.1
  851.1 53.2 all-gather.4
where the time goes:
time: 1020 us; the launch traced here: 1010 us
  waiting for transfers between devices  376 us (37%)
  matrix products  315 us (31%)
  other arithmetic  247 us (24%)
  local copies, waits for them, and re-layouts  28.8 us (3%)
  blocking collectives  21.4 us (2%)
  between operations  20 us (2%)
    another operation x29, other arithmetic, solve_right(): lower = jnp.linalg.cholesky(gram)  158 us
    psum x1, waiting for transfers between devices, on_device(): whole = lax.psum(partial_value, 'fsdp')  156 us
    dot_general x1, matrix products, on_device(): jnp.dot(tile.T, whole, precision=high, preferred_element_type=jnp.float32)  107 us
    dot_general x1, matrix products, on_device(): jnp.dot(whole, full_right.T, precision=high, preferred_element_type=jnp.f...  98.3 us
    another operation x6, other arithmetic, solve_right(): return jax.scipy.linalg.solve_triangular(lower, left.T, lower=True).T  81.9 us
    psum x2, waiting for transfers between devices, gram_over_rows(): return lax.psum(local_gram(left), 'tp')  71.6 us
    reduce_scatter x1, waiting for transfers between devices, on_device(): lax.psum_scatter(partial_right, 'tp', scatter_dimension=1, tiled=True)  65.2 us
    all_gather x1, waiting for transfers between devices, on_device(): lax.all_gather(basis, 'tp', axis=1, tiled=True)  57.6 us
  transfers between devices with their start and end apart: 6, of which 6 were waited for; matrix products, arithmetic and copies ran while one was open for 1% of the time, Pallas kernels for 0%

commit v1 on v0

v1 whole, which is shorter than its diff:
```python
import functools

import jax
import jax.numpy as jnp
from jax import lax
from jax.experimental import pallas as pl
from jax.experimental.pallas import tpu as pltpu
from jax.sharding import PartitionSpec as P

keep_rate = 0.95
tiny = 1e-06
highest = lax.Precision.HIGHEST
BLOCK = 128
PANEL = 8


def product(a, b, dims, precision=highest):
    return lax.dot_general(a, b, ((dims[:1], dims[1:]), ((), ())), precision=precision, preferred_element_type=jnp.float32)


def eliminate_block(m_ref):
    lanes = lax.broadcasted_iota(jnp.int32, (PANEL, BLOCK), 1)
    subs = lax.broadcasted_iota(jnp.int32, (PANEL, BLOCK), 0)
    rows = lax.broadcasted_iota(jnp.int32, (BLOCK, BLOCK), 0)
    columns = lax.broadcasted_iota(jnp.int32, (BLOCK, BLOCK), 1)
    for start in range(0, BLOCK, PANEL):
        panel = m_ref[start:start + PANEL, :]
        heads = [jnp.broadcast_to(panel[:, start + j:start + j + 1], (PANEL, BLOCK)) for j in range(PANEL)]
        for j in range(PANEL):
            head = heads[j]
            pivot = jnp.broadcast_to(head[j:j + 1, :], (PANEL, BLOCK))
            root = lax.rsqrt(pivot)
            root = root * (1.5 - 0.5 * (pivot * root) * root)
            factor = jnp.where(subs > j, head * root, 0.0)
            row = jnp.broadcast_to(panel[j:j + 1, :], (PANEL, BLOCK)) * root
            row = jnp.where(lanes == start + j, root, row)
            kept = jnp.where((lanes == start + j) & (subs > j), 0.0, panel)
            panel = jnp.where(subs == j, row, kept - factor * row)
            for later in range(j + 1, PANEL):
                scaled = jnp.broadcast_to(heads[later][j:j + 1, :], (PANEL, BLOCK)) * root
                heads[later] = heads[later] - factor * scaled
        m_ref[start:start + PANEL, :] = jnp.where(lanes > start + subs, 0.0, panel)
        stop = start + PANEL
        if stop < BLOCK:
            right = jnp.where(lanes >= stop, panel, 0.0)
            own = jnp.where((lanes > start + subs) & (lanes < stop), 0.0, panel)
            update = product(right, own, (0, 0))
            below = m_ref[stop:, :]
            fresh = (columns[stop:] >= start) & (columns[stop:] < stop)
            m_ref[stop:, :] = jnp.where(fresh, 0.0, below) - update[stop:, :]


def inverse_factor_kernel(g_ref, x_ref, m_ref):
    n = g_ref.shape[0]
    x_ref[...] = g_ref[...]
    for start in range(0, n, BLOCK):
        stop = start + BLOCK
        m_ref[...] = x_ref[start:stop, start:stop]
        eliminate_block(m_ref)
        diagonal = m_ref[...]
        x_ref[start:stop, start:stop] = diagonal
        if start > 0:
            x_ref[start:stop, :start] = product(diagonal, x_ref[start:stop, :start], (1, 0))
        if stop < n:
            right = product(diagonal, x_ref[start:stop, stop:], (1, 0))
            if start > 0:
                x_ref[stop:, :start] -= product(right, x_ref[start:stop, :start], (0, 0))
            x_ref[stop:, start:stop] = -product(right, diagonal, (0, 0))
            x_ref[stop:, stop:] -= product(right, right, (0, 0))
            x_ref[start:stop, stop:] = jnp.zeros((BLOCK, n - stop), jnp.float32)


def inverse_factor(gram):
    n = gram.shape[0]
    return pl.pallas_call(
        inverse_factor_kernel,
        out_shape=jax.ShapeDtypeStruct((n, n), jnp.float32),
        in_specs=[pl.BlockSpec(memory_space=pltpu.VMEM)],
        out_specs=pl.BlockSpec(memory_space=pltpu.VMEM),
        scratch_shapes=[pltpu.VMEM((BLOCK, BLOCK), jnp.float32)],
        cost_estimate=pl.CostEstimate(flops=2 * n * n * n * 20, bytes_accessed=8 * n * n, transcendentals=n),
        name="inverse_factor",
    )(gram)


MESH = pl.DeviceIdType.MESH


def sum_kernel(axes, sizes, g_ref, out_ref, land0, land1, sum0, sum1, send0, recv0, send1, recv1, send2, recv2, send3, recv3):
    (outer, inner), (count0, count1) = axes, sizes
    me0, me1 = lax.axis_index(outer), lax.axis_index(inner)
    rows0 = g_ref.shape[0] // count0
    rows1 = rows0 // count1

    def peer(axis, me, count, step):
        return {axis: lax.rem(me + step, count)}

    barrier = pltpu.get_barrier_semaphore()
    for axis, me, count in ((outer, me0, count0), (inner, me1, count1)):
        for step in range(1, count):
            pl.semaphore_signal(barrier, inc=1, device_id=peer(axis, me, count, step), device_id_type=MESH)
    pl.semaphore_wait(barrier, count0 + count1 - 2)

    def rows(index, size):
        return pl.ds(pl.multiple_of(index * size, size), size)

    def scatter(axis, me, count, size, source, land, send, recv):
        copies = []
        for step in range(1, count):
            target = lax.rem(me + step, count)
            copies.append(pltpu.make_async_remote_copy(
                src_ref=source.at[rows(target, size)], dst_ref=land.at[step], send_sem=send.at[step],
                recv_sem=recv.at[step], device_id={axis: target}, device_id_type=MESH))
        for copy in copies:
            copy.start()
        return copies

    def gather(axis, me, count, size, source, base, send, recv):
        copies = []
        for step in range(1, count):
            target = lax.rem(me + step, count)
            copies.append(pltpu.make_async_remote_copy(
                src_ref=source, dst_ref=out_ref.at[pl.ds(pl.multiple_of(base, size), size)], send_sem=send.at[step],
                recv_sem=recv.at[step], device_id={axis: target}, device_id_type=MESH))
        for copy in copies:
            copy.start()
        return copies

    first = scatter(outer, me0, count0, rows0, g_ref, land0, send0, recv0)
    total = g_ref[rows(me0, rows0), :]
    for step in range(1, count0):
        first[step - 1].wait_recv()
        total = total + land0[step]
    sum0[...] = total
    second = scatter(inner, me1, count1, rows1, sum0, land1, send1, recv1)
    total = sum0[rows(me1, rows1), :]
    for step in range(1, count1):
        second[step - 1].wait_recv()
        total = total + land1[step]
    sum1[...] = total
    place = me0 * rows0 + me1 * rows1
    third = gather(inner, me1, count1, rows1, sum1, place, send2, recv2)
    out_ref[pl.ds(pl.multiple_of(place, rows1), rows1), :] = total
    for copy in third:
        copy.wait_recv()
    base = me0 * rows0
    fourth = gather(outer, me0, count0, rows0, out_ref.at[rows(me0, rows0)], base, send3, recv3)
    for copy in fourth:
        copy.wait_recv()
    for copy in first + second + third + fourth:
        copy.wait_send()


def sum_over_devices(gram, axes):
    n, columns = gram.shape
    sizes = tuple(lax.axis_size(axis) for axis in axes)
    if max(sizes) > 8 or n % (8 * sizes[0] * sizes[1]):
        return lax.psum(gram, axes)
    rows0 = n // sizes[0]
    rows1 = rows0 // sizes[1]
    semaphores = [pltpu.SemaphoreType.DMA((size,)) for size in (sizes[0], sizes[0], sizes[1], sizes[1], sizes[1], sizes[1], sizes[0], sizes[0])]
    return pl.pallas_call(
        functools.partial(sum_kernel, axes, sizes),
        out_shape=jax.ShapeDtypeStruct((n, columns), jnp.float32),
        in_specs=[pl.BlockSpec(memory_space=pltpu.VMEM)],
        out_specs=pl.BlockSpec(memory_space=pltpu.VMEM),
        scratch_shapes=[
            pltpu.VMEM((sizes[0], rows0, columns), jnp.float32),
            pltpu.VMEM((sizes[1], rows1, columns), jnp.float32),
            pltpu.VMEM((rows0, columns), jnp.float32),
            pltpu.VMEM((rows1, columns), jnp.float32),
        ] + semaphores,
        compiler_params=pltpu.CompilerParams(collective_id=0, has_side_effects=True),
        cost_estimate=pl.CostEstimate(flops=n * columns * 2, bytes_accessed=8 * n * columns, transcendentals=0),
        name="sum_over_devices",
    )(gram)


def on_device(momentum, gradient, basis):
    tile = momentum + gradient.astype(jnp.float32)
    partial_sketch = product(tile, lax.all_gather(basis, "tp", axis=1, tiled=True), (1, 0))
    own = lax.psum_scatter(partial_sketch, "fsdp", scatter_dimension=0, tiled=True)
    gram = sum_over_devices(product(own, own, (0, 0)), ("fsdp", "tp"))
    half = own.shape[0] // 2
    gram, own_later = lax.optimization_barrier((gram, own[:half]))
    sketch = lax.all_gather(own_later, "fsdp", axis=0)
    inverse = inverse_factor(gram)
    own_first = product(own, inverse, (1, 1))
    gram = sum_over_devices(product(own_first, own_first, (0, 0)), ("fsdp", "tp"))
    gram, first_later = lax.optimization_barrier((gram, own_first[half:]))
    later_half = lax.all_gather(first_later, "fsdp", axis=0)
    second = inverse_factor(gram)
    own_left = product(own_first, second, (1, 1))
    early_half = lax.dot_general(sketch, inverse, (((2,), (1,)), ((), ())), precision=highest, preferred_element_type=jnp.float32)
    first = jnp.concatenate([early_half, later_half], axis=1).reshape(tile.shape[0], -1)
    left = product(first, second, (1, 1))
    partial_right = product(tile, left, (0, 0), lax.Precision.HIGH)
    mine = lax.psum_scatter(partial_right, "tp", scatter_dimension=1, tiled=True)
    squares = lax.psum(jnp.sum(mine * mine, axis=0), "fsdp")
    new_basis = mine / jnp.sqrt(squares + tiny)[None, :]
    full_right = lax.all_gather(mine, "tp", axis=1, tiled=True)
    new_momentum = tile - (1.0 - keep_rate) * product(left, full_right, (1, 1), lax.Precision.DEFAULT)
    return (new_momentum, new_basis, own_left)


def solution(mesh):
    placed = (P("tp", "fsdp"), P("tp", "fsdp"), P("fsdp", "tp"))
    return jax.shard_map(
        on_device,
        mesh=mesh,
        in_specs=placed,
        out_specs=(P("tp", "fsdp"), P("fsdp", "tp"), P(("tp", "fsdp"), None)),
        check_vma=False,
    )
```

time: 1020 us -> 626 us (0.61)
  other arithmetic: 247 us -> 7 us
  Pallas kernels: 0 us -> 185 us
  matrix products: 315 us -> 135 us
  waiting for transfers between devices: 376 us -> 254 us
  local copies, waits for them, and re-layouts: 28.8 us -> 4.48 us
    another operation x35 -> x0, other arithmetic: 240 us -> none  [the longest x29 158 us: solve_right(): lower = jnp.linalg.cholesky(gram)]
    psum x3 -> x0, waiting for transfers between devices: 228 us -> none  [the longest x1 156 us: on_device(): whole = lax.psum(partial_value, 'fsdp')]
    pallas_call x0 -> x4, Pallas kernels: none -> 185 us  [the longest x2 109 us: sum_over_devices(): pl.pallas_call(functools.partial(sum_kernel, axes, sizes), out_shape=jax....]
    dot_general x5 -> x9, matrix products: 279 us -> 135 us  [the longest x8 129 us: product(): lax.dot_general(a, b, ((dims[:1], dims[1:]), ((), ())), precision=precisi...]
    reduce_scatter x0 -> x1, waiting for transfers between devices: none -> 88.4 us  [on_device(): lax.psum_scatter(partial_sketch, 'fsdp', scatter_dimension=0, tiled=True)]
    another operation x26 -> x0, matrix products: 36.9 us -> none  [the longest x14 29.5 us: solve_right(): return jax.scipy.linalg.solve_triangular(lower, left.T, lower=True).T]
    another operation x35 -> x0, local copies, waits for them, and re-layouts: 19.9 us -> none  [the longest x27 19.6 us: solve_right(): return jax.scipy.linalg.solve_triangular(lower, left.T, lower=True).T]
    all_gather x0 -> x2, waiting for transfers between devices: none -> 17.2 us  [the longest x1 17.2 us: on_device(): later_half = lax.all_gather(first_later, 'fsdp', axis=0)]
  transfers between devices with their start and end apart: 6 -> 6, of which waited for: 6 -> 5; matrix products, arithmetic and copies ran while one was open for 1% -> 3% of each run, Pallas kernels for 0% -> 22%
where the time goes in v1:
time: 626 us; the launch traced here: 621 us
  waiting for transfers between devices  254 us (41%)
  Pallas kernels  185 us (30%)
  matrix products  135 us (22%)
  blocking collectives  21.4 us (3%)
  between operations  14.4 us (2%)
  other arithmetic  7 us (1%)
    dot_general x8, matrix products, product(): lax.dot_general(a, b, ((dims[:1], dims[1:]), ((), ())), precision=precisi...  129 us
    pallas_call x2, Pallas kernels, sum_over_devices(): pl.pallas_call(functools.partial(sum_kernel, axes, sizes), out_shape=jax....  109 us
    reduce_scatter x1, waiting for transfers between devices, on_device(): lax.psum_scatter(partial_sketch, 'fsdp', scatter_dimension=0, tiled=True)  88.4 us
    pallas_call x2, Pallas kernels, inverse_factor(): pl.pallas_call(inverse_factor_kernel, out_shape=jax.ShapeDtypeStruct((n,...  75.7 us
    reduce_scatter x1, waiting for transfers between devices, on_device(): lax.psum_scatter(partial_right, 'tp', scatter_dimension=1, tiled=True)  63.6 us
    all_gather x1, waiting for transfers between devices, on_device(): lax.all_gather(basis, 'tp', axis=1, tiled=True)  57.6 us
    all_gather x1, waiting for transfers between devices, on_device(): full_right = lax.all_gather(mine, 'tp', axis=1, tiled=True)  26.6 us
    psum x1, blocking collectives, on_device(): squares = lax.psum(jnp.sum(mine * mine, axis=0), 'fsdp')  21.4 us
  transfers between devices with their start and end apart: 6, of which 5 were waited for; matrix products, arithmetic and copies ran while one was open for 3% of the time, Pallas kernels for 22%

profile of v1, /device:TPU:0, one launch (start us, length us, event | category | flops | bytes accessed | tf_op | source)
XLA Modules:
  0.0 621.0 jit_solution(13784509738666057817)
XLA Ops:
  7.2 0.0 all-gather.7.cloned.1.call-start
  7.2 0.7 all-gather.7.cloned.1.call-update
  7.9 0.0 reduce-scatter.3.cloned.1.call-start
  7.9 57.6 %all-gather.7.cloned.1.call-done = f32[3584,512]{1,0:T(8,128)} async-done(((f32[3584,128]{1,0:T(8,128)}), f32[3584,512]{1,0:T(8,128)}) %all-gather.7.cloned.1.call-update) | async-done | bytes 7340048 | tf_op jit(solution)/shard_map/all_gather | solution.py:181
  65.6 53.8 %fusion.1 = f32[2048,512]{1,0:T(8,128)} fusion(f32[3584,512]{1,0:T(8,128)} %all-gather.7.cloned.1.call-done, f32[2048,3584]{1,0:T(8,128)} %param.3, bf16[2048,3584]{1,0:T(8,128)(2,1)} %param.4), kind=kOutput, calls=%fused_computation.3 | convolution fusion | flops 45111836672 | bytes 55574528 | tf_op jit(solution)/shard_map/dot_general | solution.py:18
  119.4 0.0 all-gather.11.cloned.1.call-start
  119.4 88.4 %reduce-scatter.3.cloned.1.call-done = f32[256,512]{1,0:T(8,128)} async-done(((f32[2048,512]{1,0:T(8,128)}), f32[256,512]{1,0:T(8,128)}) %reduce-scatter.3.cloned.1.call-update) | async-done | bytes 524304 | tf_op jit(solution)/shard_map/reduce_scatter | solution.py:182
  207.8 3.2 fusion.4.g_ref
  211.0 48.1 %sum_over_devices.2.g_ref = f32[512,512]{1,0:T(8,128)} custom-call(f32[512,512]{1,0:T(8,128)} %fusion.4.g_ref), custom_call_target="tpu_custom_call" | custom-call | flops 524288 | bytes 2097152 | tf_op jit(solution)/shard_map/sum_over_devices/pallas_call | solution.py:162
  259.1 1.7 slice.8
  260.8 0.2 all-gather.13.cloned.1.call-start
  261.1 38.0 %inverse_factor.2 = f32[512,512]{1,0:T(8,128)} custom-call(f32[512,512]{1,0:T(8,128)} %sum_over_devices.2.g_ref), custom_call_target="tpu_custom_call" | custom-call | flops 5368709120 | bytes 2097152 | tf_op jit(solution)/shard_map/inverse_factor/pallas_call | solution.py:75
  299.0 2.4 fusion.5
  301.4 0.7 slice.9
  302.1 2.0 fusion.6.g_ref
  304.1 60.8 %sum_over_devices.3.g_ref = f32[512,512]{1,0:T(8,128)} custom-call(f32[512,512]{1,0:T(8,128)} %fusion.6.g_ref), custom_call_target="tpu_custom_call" | custom-call | flops 524288 | bytes 2097152 | tf_op jit(solution)/shard_map/sum_over_devices/pallas_call | solution.py:162
  364.9 0.0 reduce-scatter.5.cloned.1.call-start
  365.0 37.7 %inverse_factor.3 = f32[512,512]{1,0:T(8,128)} custom-call(f32[512,512]{1,0:T(8,128)} %sum_over_devices.3.g_ref), custom_call_target="tpu_custom_call" | custom-call | flops 5368709120 | bytes 2097152 | tf_op jit(solution)/shard_map/inverse_factor/pallas_call | solution.py:75
  402.7 5.4 fusion.2
  408.1 17.2 %all-gather.13.cloned.1.call-done = f32[1024,512]{1,0:T(8,128)} async-done(((f32[128,512]{1,0:T(8,128)}), f32[1024,512]{1,0:T(8,128)}) %all-gather.13.cloned.1.call-update) | async-done | bytes 2097168 | tf_op jit(solution)/shard_map/all_gather | solution.py:191
  425.3 2.1 pad_maximum_fusion
  427.5 7.1 %fusion.7 = f32[2048,512]{1,0:T(8,128)S(1)} fusion(f32[2048,512]{1,0:T(8,128)S(1)} %bitcast.22, f32[512,512]{1,0:T(8,128)S(1)} %copy-done.2), kind=kOutput, calls=%fused_computation.13 | convolution fusion | flops 6442450944 | bytes 9437184 | tf_op jit(solution)/shard_map/dot_general | solution.py:18
  434.6 2.1 copy-done
  436.7 29.3 %fusion = f32[3584,512]{1,0:T(8,128)} fusion(f32[2048,512]{1,0:T(8,128)S(1)} %fusion.7, f32[2048,3584]{1,0:T(8,128)} %param.3, bf16[2048,3584]{1,0:T(8,128)(2,1)} %param.4), kind=kOutput, calls=%fused_computation.2 | convolution fusion | flops 22563258368 | bytes 55574528 | tf_op jit(solution)/shard_map/dot_general | solution.py:18
  466.0 0.0 all-gather.9.cloned.1.call-start
  466.0 63.6 %reduce-scatter.5.cloned.1.call-done = f32[3584,128]{1,0:T(8,128)} async-done(((f32[3584,512]{1,0:T(8,128)}), f32[3584,128]{1,0:T(8,128)}) %reduce-scatter.5.cloned.1.call-update) | async-done | bytes 1835024 | tf_op jit(solution)/shard_map/reduce_scatter | solution.py:198
  529.7 1.9 fusion.8
  531.5 2.0 multiply_reduce_fusion
  533.5 21.4 %psum.7 = f32[128]{0:T(128)S(1)} all-reduce(f32[128]{0:T(128)S(1)} %multiply_reduce_fusion), channel_id=1, replica_groups=mesh['tp'=4,'fsdp'=8] {'fsdp'}, use_global_device_ids=true, to_apply=%region_3.0 | all-reduce | flops 128 | bytes 1024 | tf_op jit(solution)/shard_map/psum | solution.py:199
  554.9 2.9 broadcast_divide_fusion
  557.7 26.6 %all-gather.9.cloned.1.call-done = f32[3584,512]{1,0:T(8,128)} async-done(((f32[3584,128]{1,0:T(8,128)}), f32[3584,512]{1,0:T(8,128)}) %all-gather.9.cloned.1.call-update) | async-done | bytes 7340048 | tf_op jit(solution)/shard_map/all_gather | solution.py:201
  584.4 29.6 %multiply_subtract_fusion = f32[2048,3584]{1,0:T(8,128)} fusion(f32[2048,512]{1,0:T(8,128)} %copy-done, f32[3584,512]{1,0:T(8,128)} %all-gather.9.cloned.1.call-done, f32[2048,3584]{1,0:T(8,128)} %param.3, bf16[2048,3584]{1,0:T(8,128)(2,1)} %param.4), kind=kOutput, calls=%fused_computation | convolution fusion | flops 7545552896 | bytes 84934656 | tf_op jit(solution)/shard_map/dot_general | solution.py:18
  (14 shorter events, 0.1 us)
Async XLA Ops:
  7.2 58.4 %all-gather.7.cloned.1.call-start = ((), (), s32[]{:S(2)}) async-start(), calls=%async_computation.2 | async-start | bytes 9175040 | tf_op jit(solution)/shard_map/all_gather | solution.py:181
  7.9 199.9 %reduce-scatter.3.cloned.1.call-start = ((), (), s32[]{:S(2)}) async-start(), calls=%async_computation.3 | async-start | bytes 4718592 | tf_op jit(solution)/shard_map/reduce_scatter | solution.py:182
  119.4 283.4 %all-gather.11.cloned.1.call-start = ((), (), s32[]{:S(2)}) async-start(), calls=%async_computation.6 | async-start | bytes 2359296 | tf_op jit(solution)/shard_map/all_gather | solution.py:186
  260.8 38.2 %copy-start.1 = (f32[256,512]{1,0:T(8,128)S(1)}, f32[256,512]{1,0:T(8,128)}, u32[]{:S(2)}) copy-start(f32[256,512]{1,0:T(8,128)} %reduce-scatter.3.cloned.1.call-done) | copy-start | bytes 1572868
  260.8 164.5 %all-gather.13.cloned.1.call-start = ((), (), s32[]{:S(2)}) async-start(), calls=%async_computation.7 | async-start | bytes 2359296 | tf_op jit(solution)/shard_map/all_gather | solution.py:191
  364.9 164.7 %reduce-scatter.5.cloned.1.call-start = ((), (), s32[]{:S(2)}) async-start(), calls=%async_computation.4 | async-start | bytes 9175040 | tf_op jit(solution)/shard_map/reduce_scatter | solution.py:198
  425.3 2.2 copy-start.2
  434.6 2.1 copy-start
  466.0 63.7 %copy-start.3 = (f32[512,512]{1,0:T(8,128)S(1)}, f32[512,512]{1,0:T(8,128)}, u32[]{:S(2)}) copy-start(f32[512,512]{1,0:T(8,128)} %inverse_factor.3) | copy-start | bytes 3145732
  466.0 118.4 %all-gather.9.cloned.1.call-start = ((), (), s32[]{:S(2)}) async-start(), calls=%async_computation.5 | async-start | bytes 9175040 | tf_op jit(solution)/shard_map/all_gather | solution.py:201
Sparse Core Ops, SparseCore 0:
  9.5 55.9 all-gather.6
  119.5 88.2 reduce-scatter.2
  260.9 60.7 all-gather.10
  365.1 60.2 all-gather.12
  466.1 63.4 reduce-scatter.4
  531.0 53.2 all-gather.8

commit v2 on v1

--- a/solution.py
+++ b/solution.py
@@ -178,7 +178,10 @@
 
 def on_device(momentum, gradient, basis):
     tile = momentum + gradient.astype(jnp.float32)
-    partial_sketch = product(tile, lax.all_gather(basis, "tp", axis=1, tiled=True), (1, 0))
+    depth = tile.shape[1] // 2
+    early = lax.all_gather(basis[:depth], "tp", axis=1, tiled=True)
+    late = lax.all_gather(basis[depth:], "tp", axis=1, tiled=True)
+    partial_sketch = product(tile[:, :depth], early, (1, 0)) + product(tile[:, depth:], late, (1, 0))
     own = lax.psum_scatter(partial_sketch, "fsdp", scatter_dimension=0, tiled=True)
     gram = sum_over_devices(product(own, own, (0, 0)), ("fsdp", "tp"))
     half = own.shape[0] // 2
@@ -199,7 +202,7 @@
     squares = lax.psum(jnp.sum(mine * mine, axis=0), "fsdp")
     new_basis = mine / jnp.sqrt(squares + tiny)[None, :]
     full_right = lax.all_gather(mine, "tp", axis=1, tiled=True)
-    new_momentum = tile - (1.0 - keep_rate) * product(left, full_right, (1, 1), lax.Precision.DEFAULT)
+    new_momentum = tile - product(left, (1.0 - keep_rate) * full_right, (1, 1), lax.Precision.DEFAULT)
     return (new_momentum, new_basis, own_left)
 
 

time: 626 us -> 621 us (level)
  waiting for transfers between devices: 254 us -> 212 us
  other arithmetic: 7 us -> 30.4 us
  Pallas kernels: 185 us -> 197 us
    all_gather x1 -> x2, waiting for transfers between devices: 57.6 us -> 14.1 us  [the longest x1 8.22 us: on_device(): late = lax.all_gather(basis[depth:], 'tp', axis=1, tiled=True)]
    add x0 -> x1, other arithmetic: none -> 25.8 us  [on_device(): tile = momentum + gradient.astype(jnp.float32)]
    pallas_call x2, Pallas kernels: 75.7 us -> 88.3 us  [inverse_factor(): pl.pallas_call(inverse_factor_kernel, out_shape=jax.ShapeDtypeStruct((n,...]
    dot_general x8 -> x9, matrix products: 129 us -> 129 us  [product(): lax.dot_general(a, b, ((dims[:1], dims[1:]), ((), ())), precision=precisi...]
  transfers between devices with their start and end apart: 6 -> 7, of which waited for: 5 -> 6; matrix products, arithmetic and copies ran while one was open for 3% -> 11% of each run, Pallas kernels for 22% -> 24%
where the time goes in v2:
time: 621 us; the launch traced here: 618 us
  waiting for transfers between devices  212 us (34%)
  Pallas kernels  197 us (32%)
  matrix products  135 us (22%)
  other arithmetic  30.4 us (5%)
  blocking collectives  21.6 us (3%)
  between operations  14.4 us (2%)
  local copies, waits for them, and re-layouts  6.33 us (1%)
    dot_general x9, matrix products, product(): lax.dot_general(a, b, ((dims[:1], dims[1:]), ((), ())), precision=precisi...  129 us
    pallas_call x2, Pallas kernels, sum_over_devices(): pl.pallas_call(functools.partial(sum_kernel, axes, sizes), out_shape=jax....  109 us
    pallas_call x2, Pallas kernels, inverse_factor(): pl.pallas_call(inverse_factor_kernel, out_shape=jax.ShapeDtypeStruct((n,...  88.3 us
    reduce_scatter x1, waiting for transfers between devices, on_device(): lax.psum_scatter(partial_sketch, 'fsdp', scatter_dimension=0, tiled=True)  88.2 us
    reduce_scatter x1, waiting for transfers between devices, on_device(): lax.psum_scatter(partial_right, 'tp', scatter_dimension=1, tiled=True)  63.4 us
    all_gather x1, waiting for transfers between devices, on_device(): full_right = lax.all_gather(mine, 'tp', axis=1, tiled=True)  29.6 us
    add x1, other arithmetic, on_device(): tile = momentum + gradient.astype(jnp.float32)  25.8 us
    psum x1, blocking collectives, on_device(): squares = lax.psum(jnp.sum(mine * mine, axis=0), 'fsdp')  21.6 us
  transfers between devices with their start and end apart: 7, of which 6 were waited for; matrix products, arithmetic and copies ran while one was open for 11% of the time, Pallas kernels for 24%

profile of v2, /device:TPU:0, one launch (start us, length us, event | category | flops | bytes accessed | tf_op | source)
XLA Modules:
  0.0 617.7 jit_solution(10155890692095974947)
XLA Ops:
  7.2 2.8 fusion.12
  10.1 0.7 all-gather.8.cloned.1.call-update
  10.8 25.8 %convert_add_fusion = f32[2048,3584]{1,0:T(8,128)} fusion(f32[2048,3584]{1,0:T(8,128)} %param.3, bf16[2048,3584]{1,0:T(8,128)(2,1)} %param.4), kind=kLoop, calls=%fused_computation | loop fusion | flops 14680064 | bytes 73400320 | tf_op jit(solution)/shard_map/add | solution.py:180
  36.6 8.2 %all-gather.10.cloned.1.call-done = f32[1792,512]{1,0:T(8,128)} async-done(((f32[1792,128]{1,0:T(8,128)}), f32[1792,512]{1,0:T(8,128)}) %all-gather.10.cloned.1.call-update) | async-done | bytes 3670032 | tf_op jit(solution)/shard_map/all_gather | solution.py:183
  44.9 28.2 %fusion = f32[2048,512]{1,0:T(8,128)} fusion(f32[1792,512]{1,0:T(8,128)} %all-gather.10.cloned.1.call-done, f32[2048,3584]{1,0:T(8,128)} %convert_add_fusion), kind=kOutput, calls=%fused_computation.2 | convolution fusion | flops 22548578304 | bytes 22544384 | tf_op jit(solution)/shard_map/dot_general | solution.py:18
  73.1 5.9 all-gather.8.cloned.1.call-done
  79.0 28.5 %fusion.6 = f32[2048,512]{1,0:T(8,128)} fusion(f32[2048,512]{1,0:T(8,128)} %fusion, f32[1792,512]{1,0:T(8,128)} %all-gather.8.cloned.1.call-done, f32[2048,3584]{1,0:T(8,128)} %convert_add_fusion), kind=kOutput, calls=%fused_computation.9 | convolution fusion | flops 22549626880 | bytes 26738688 | tf_op jit(solution)/shard_map/dot_general | solution.py:18
  107.5 0.3 all-gather.14.cloned.1.call-start
  107.9 88.2 %reduce-scatter.3.cloned.1.call-done = f32[256,512]{1,0:T(8,128)} async-done(((f32[2048,512]{1,0:T(8,128)}), f32[256,512]{1,0:T(8,128)}) %reduce-scatter.3.cloned.1.call-update) | async-done | bytes 524304 | tf_op jit(solution)/shard_map/reduce_scatter | solution.py:185
  196.1 3.3 fusion.13.g_ref
  199.3 48.1 %sum_over_devices.2.g_ref = f32[512,512]{1,0:T(8,128)} custom-call(f32[512,512]{1,0:T(8,128)} %fusion.13.g_ref), custom_call_target="tpu_custom_call" | custom-call | flops 524288 | bytes 2097152 | tf_op jit(solution)/shard_map/sum_over_devices/pallas_call | solution.py:162
  247.4 0.7 slice.26
  248.2 0.0 all-gather.16.cloned.1.call-start
  248.2 50.2 %inverse_factor.2 = f32[512,512]{1,0:T(8,128)} custom-call(f32[512,512]{1,0:T(8,128)} %sum_over_devices.2.g_ref), custom_call_target="tpu_custom_call" | custom-call | flops 5368709120 | bytes 2097152 | tf_op jit(solution)/shard_map/inverse_factor/pallas_call | solution.py:75
  298.5 2.3 fusion.14
  300.8 0.7 slice.27
  301.5 2.0 fusion.15.g_ref
  303.5 60.8 %sum_over_devices.3.g_ref = f32[512,512]{1,0:T(8,128)} custom-call(f32[512,512]{1,0:T(8,128)} %fusion.15.g_ref), custom_call_target="tpu_custom_call" | custom-call | flops 524288 | bytes 2097152 | tf_op jit(solution)/shard_map/sum_over_devices/pallas_call | solution.py:162
  364.4 38.1 %inverse_factor.3 = f32[512,512]{1,0:T(8,128)} custom-call(f32[512,512]{1,0:T(8,128)} %sum_over_devices.3.g_ref), custom_call_target="tpu_custom_call" | custom-call | flops 5368709120 | bytes 2097152 | tf_op jit(solution)/shard_map/inverse_factor/pallas_call | solution.py:75
  402.5 6.4 %fusion.9 = f32[8,128,512]{2,1,0:T(8,128)} fusion(f32[8,128,512]{2,1,0:T(8,128)} %bitcast.23, f32[512,512]{1,0:T(8,128)S(1)} %copy-done.3), kind=kOutput, calls=%fused_computation.11 | convolution fusion | flops 3221225472 | bytes 5242880 | tf_op jit(solution)/shard_map/dot_general | solution.py:197
  408.9 15.8 %all-gather.16.cloned.1.call-done = f32[1024,512]{1,0:T(8,128)} async-done(((f32[128,512]{1,0:T(8,128)}), f32[1024,512]{1,0:T(8,128)}) %all-gather.16.cloned.1.call-update) | async-done | bytes 2097168 | tf_op jit(solution)/shard_map/all_gather | solution.py:194
  424.7 2.8 pad_maximum_fusion
  427.5 7.6 %fusion.16 = f32[2048,512]{1,0:T(8,128)S(1)} fusion(f32[2048,512]{1,0:T(8,128)S(1)} %bitcast.22, f32[512,512]{1,0:T(8,128)S(1)} %copy-done.4), kind=kOutput, calls=%fused_computation.20 | convolution fusion | flops 6442450944 | bytes 9437184 | tf_op jit(solution)/shard_map/dot_general | solution.py:18
  435.1 2.1 copy-done
  437.2 28.4 %fusion.17 = f32[3584,512]{1,0:T(8,128)} fusion(f32[2048,3584]{1,0:T(8,128)} %convert_add_fusion, f32[2048,512]{1,0:T(8,128)S(1)} %fusion.16), kind=kOutput, calls=%fused_computation.21 | convolution fusion | flops 22548578304 | bytes 40894464 | tf_op jit(solution)/shard_map/dot_general | solution.py:18
  465.6 63.4 %reduce-scatter.5.cloned.1.call-done = f32[3584,128]{1,0:T(8,128)} async-done(((f32[3584,512]{1,0:T(8,128)}), f32[3584,128]{1,0:T(8,128)}) %reduce-scatter.5.cloned.1.call-update) | async-done | bytes 1835024 | tf_op jit(solution)/shard_map/reduce_scatter | solution.py:201
  529.0 1.9 fusion.18
  530.9 0.5 multiply_reduce_fusion
  531.4 21.6 %psum.7 = f32[128]{0:T(128)S(1)} all-reduce(f32[128]{0:T(128)S(1)} %multiply_reduce_fusion), channel_id=1, replica_groups=mesh['tp'=4,'fsdp'=8] {'fsdp'}, use_global_device_ids=true, to_apply=%region_3.0 | all-reduce | flops 128 | bytes 1024 | tf_op jit(solution)/shard_map/psum | solution.py:202
  553.0 1.4 broadcast_divide_fusion
  554.3 29.6 %all-gather.12.cloned.1.call-done = f32[3584,512]{1,0:T(8,128)} async-done(((f32[3584,128]{1,0:T(8,128)}), f32[3584,512]{1,0:T(8,128)}) %all-gather.12.cloned.1.call-update) | async-done | bytes 7340048 | tf_op jit(solution)/shard_map/all_gather | solution.py:204
  583.9 26.8 %convolution_subtract_fusion = f32[2048,3584]{1,0:T(8,128)} fusion(f32[2048,3584]{1,0:T(8,128)} %convert_add_fusion, f32[2048,512]{1,0:T(8,128)} %copy-done, f32[3584,512]{1,0:T(8,128)} %all-gather.12.cloned.1.call-done), kind=kOutput, calls=%fused_computation.1 | convolution fusion | flops 7525367808 | bytes 70254592 | tf_op jit(solution)/shard_map/dot_general | solution.py:18
  (22 shorter events, 0.3 us)
Async XLA Ops:
  7.2 37.7 %all-gather.10.cloned.1.call-start = ((), (), s32[]{:S(2)}) async-start(), calls=%async_computation.3 | async-start | bytes 4587520 | tf_op jit(solution)/shard_map/all_gather | solution.py:183
  10.0 68.9 %all-gather.8.cloned.1.call-start = ((), (), s32[]{:S(2)}) async-start(), calls=%async_computation.2 | async-start | bytes 4587520 | tf_op jit(solution)/shard_map/all_gather | solution.py:182
  10.8 185.3 %reduce-scatter.3.cloned.1.call-start = ((), (), s32[]{:S(2)}) async-start(), calls=%async_computation.4 | async-start | bytes 4718592 | tf_op jit(solution)/shard_map/reduce_scatter | solution.py:185
  107.5 294.9 %all-gather.14.cloned.1.call-start = ((), (), s32[]{:S(2)}) async-start(), calls=%async_computation.7 | async-start | bytes 2359296 | tf_op jit(solution)/shard_map/all_gather | solution.py:189
  196.1 51.3 %copy-start.2 = (f32[256,512]{1,0:T(8,128)S(1)}, f32[256,512]{1,0:T(8,128)}, u32[]{:S(2)}) copy-start(f32[256,512]{1,0:T(8,128)} %reduce-scatter.3.cloned.1.call-done) | copy-start | bytes 1572868
  248.2 176.5 %all-gather.16.cloned.1.call-start = ((), (), s32[]{:S(2)}) async-start(), calls=%async_computation.8 | async-start | bytes 2359296 | tf_op jit(solution)/shard_map/all_gather | solution.py:194
  364.3 38.1 %copy-start.3 = (f32[512,512]{1,0:T(8,128)S(1)}, f32[512,512]{1,0:T(8,128)}, u32[]{:S(2)}) copy-start(f32[512,512]{1,0:T(8,128)} %inverse_factor.2) | copy-start | bytes 3145732
  364.3 164.7 %reduce-scatter.5.cloned.1.call-start = ((), (), s32[]{:S(2)}) async-start(), calls=%async_computation.5 | async-start | bytes 9175040 | tf_op jit(solution)/shard_map/reduce_scatter | solution.py:201
  424.7 2.8 copy-start.4
  435.1 2.1 copy-start
  465.6 118.3 %all-gather.12.cloned.1.call-start = ((), (), s32[]{:S(2)}) async-start(), calls=%async_computation.6 | async-start | bytes 9175040 | tf_op jit(solution)/shard_map/all_gather | solution.py:204
  529.0 1.9 copy-start.1
Sparse Core Ops, SparseCore 0:
  10.2 34.6 all-gather.9
  47.0 31.9 all-gather.7
  107.7 88.3 reduce-scatter.2
  248.3 60.8 all-gather.13
  364.5 60.1 all-gather.15
  465.7 63.2 reduce-scatter.4
  530.6 53.2 all-gather.11
